TPU v7x, 32 devices: a whole 2x2x4 slice. The times are simulated.
32 devices in a mesh: segment: 2 (over core), expert: 8 (over z, y), dp: 2 (over x).
Axes of the slice: x: 2, y: 2, z: 4, core: 2. Of those that a mesh axis runs over, the one named last changes fastest.
Arguments:
- moe_input: bfloat16 [2, 1024, 2688], P('segment', 'expert', 'dp'), may hold values from -64 to 64
- norm_gain: float32 [2688], replicated, may hold values from 0.1 to 1.9
- routes: int32 [2, 1024, 6], P('segment', 'expert'), may hold values from 0 to 15, all different within a row; in each aligned block of 128 rows (0 to 127, 128 to 255, ..., all dimensions but the last counted through in order) at most 54 rows name the same one
- route_scores: float32 [2, 1024, 6], P('segment', 'expert'), may hold values from -8 to 8
- w_up: bfloat16 [16, 2688, 1856], P('expert', None, 'dp'), may hold values from -0.125 to 0.125
- w_down: bfloat16 [16, 1856, 2688], P('expert', None, 'dp'), may hold values from -0.125 to 0.125
- queries: bfloat16 [2, 1024, 2048], P('segment', 'expert', 'dp'), may hold values from -100 to 100
- keys: bfloat16 [2, 1024, 256], P('segment', 'expert'), may hold values from -6 to 6
- values: bfloat16 [2, 1024, 256], P('segment', 'expert'), may hold values from -6 to 6
- out_grad: bfloat16 [2, 1024, 2688], P('segment', 'expert'), may hold values from -6 to 6
- w_query: bfloat16 [2688, 2048], P(None, 'dp'), may hold values from -0.125 to 0.125
- w_key: bfloat16 [2688, 256], replicated, may hold values from -0.125 to 0.125
- w_value: bfloat16 [2688, 256], replicated, may hold values from -0.125 to 0.125
- w_out: bfloat16 [2048, 2688], P('dp'), may hold values from -0.125 to 0.125
Outputs:
- moe_next: bfloat16 [2, 1024, 2688], P('segment', 'expert', 'dp')
- grad_prev: bfloat16 [2, 1024, 2688], P('segment', 'expert', 'dp')
Inputs may be any that keep to these rules, and one draw needn't show every extreme that they name: `routes`: each row names 6 different experts. Among the 128 rows of one sequence no expert is named more than 54 times, a bound that some block reaches; every expert is named by some row.
All inputs are finite; a program needn't handle non-finite values.
Results may differ from a plain program's by a relative error of at most 0.028.
Values may be sent and summed in bfloat16 or wider, within the bound.
No kernel may reach another device: no remote copies, remote signals or barrier semaphores. Data moves between devices by JAX's collectives and lax.ppermute only.
A program may use at most 128 MiB of HBM per device.

v0:
```python
import jax
import jax.numpy as jnp
from jax import lax
from jax.sharding import PartitionSpec as P

D = 2688
HEADS = 16
KV_HEADS = 2
HEAD_DIM = 128
TOPK = 6
NORM_EPSILON = 1e-05


def partner(block, axis, distance):
    count = lax.axis_size(axis)
    route = []
    for low in range(count):
        high = low | 1 << distance
        if high != low and high < count:
            route += [(low, high), (high, low)]
    return lax.ppermute(block, axis, route)


def attention_grad(queries, keys, values, out_grad, w_query, w_key, w_value, w_out, block_index):
    token_count = queries.shape[0]
    query_width = queries.shape[1]
    heads_here = query_width // HEAD_DIM
    group_size = HEADS // KV_HEADS
    score_scale = HEAD_DIM ** (-0.5)
    head_group = block_index * heads_here // group_size
    kv_start = head_group * HEAD_DIM
    key_head = lax.dynamic_slice_in_dim(keys, kv_start, HEAD_DIM, 1)
    value_head = lax.dynamic_slice_in_dim(values, kv_start, HEAD_DIM, 1)
    key_weight = lax.dynamic_slice_in_dim(w_key, kv_start, HEAD_DIM, 1)
    value_weight = lax.dynamic_slice_in_dim(w_value, kv_start, HEAD_DIM, 1)
    d_attn = jnp.einsum("td,qd->tq", out_grad, w_out, preferred_element_type=jnp.float32).astype(
        jnp.bfloat16
    )
    grad_heads = d_attn.reshape(token_count, heads_here, HEAD_DIM)
    query_heads = queries.reshape(token_count, heads_here, HEAD_DIM)
    scores = (
        jnp.einsum("ihd,jd->hij", query_heads, key_head, preferred_element_type=jnp.float32)
        * score_scale
    )
    positions = jnp.arange(token_count, dtype=jnp.int32)
    causal = positions[None, :] <= positions[:, None]
    scores = jnp.where(causal[None], scores, -jnp.inf)
    peak = jnp.max(scores, axis=2, keepdims=True)
    raised = jnp.exp(scores - peak)
    attn_weights = raised / jnp.sum(raised, axis=2, keepdims=True)
    d_weights = jnp.einsum(
        "ihd,jd->hij", grad_heads, value_head, preferred_element_type=jnp.float32
    )
    row_delta = jnp.sum(attn_weights * d_weights, axis=2, keepdims=True)
    d_scores = (attn_weights * (d_weights - row_delta)).astype(jnp.bfloat16)
    d_query = (
        jnp.einsum("hij,jd->ihd", d_scores, key_head, preferred_element_type=jnp.float32)
        * score_scale
    )
    d_query = d_query.astype(jnp.bfloat16).reshape(token_count, query_width)
    d_key = (
        jnp.einsum("hij,ihd->jd", d_scores, query_heads, preferred_element_type=jnp.float32)
        * score_scale
    ).astype(jnp.bfloat16)
    d_value = jnp.einsum(
        "hij,ihd->jd",
        attn_weights.astype(jnp.bfloat16),
        grad_heads,
        preferred_element_type=jnp.float32,
    ).astype(jnp.bfloat16)
    grad_term = jnp.einsum("tq,dq->td", d_query, w_query, preferred_element_type=jnp.float32)
    grad_term = grad_term + jnp.einsum(
        "tk,dk->td", d_key, key_weight, preferred_element_type=jnp.float32
    )
    grad_term = grad_term + jnp.einsum(
        "tk,dk->td", d_value, value_weight, preferred_element_type=jnp.float32
    )
    return grad_term


def block_product(block_rows, w_up, first_feature):
    width = block_rows.shape[3]
    weight_rows = lax.dynamic_slice_in_dim(w_up, first_feature, width, 1)
    product = jnp.einsum(
        "sjcw,jwh->sjch", block_rows, weight_rows, preferred_element_type=jnp.float32
    )
    return lax.optimization_barrier(product.astype(jnp.bfloat16)).astype(jnp.float32)


def on_device(
    moe_input,
    norm_gain,
    routes,
    route_scores,
    w_up,
    w_down,
    queries,
    keys,
    values,
    out_grad,
    w_query,
    w_key,
    w_value,
    w_out,
):
    columns = lax.axis_size("expert")
    token_count = moe_input.shape[1]
    feature_share = moe_input.shape[2]
    local_experts = w_up.shape[0]
    hidden_share = w_up.shape[2]
    expert_count = local_experts * columns
    capacity = (9 * token_count * TOPK + 8 * expert_count - 1) // (8 * expert_count)
    slot_count = expert_count * capacity
    feature_index = lax.axis_index("dp")
    token_rows = moe_input[0]
    chosen_experts = routes[0]
    logits = route_scores[0]
    flat_choices = chosen_experts.reshape(-1)
    expert_hits = (
        flat_choices[:, None] == jnp.arange(expert_count, dtype=jnp.int32)[None, :]
    ).astype(jnp.int32)
    earlier = jnp.cumsum(expert_hits, axis=0) - expert_hits
    places = jnp.sum(earlier * expert_hits, axis=1).reshape(token_count, TOPK)
    targets = chosen_experts * capacity + places
    slot_ids = jnp.arange(slot_count, dtype=jnp.int32)
    signal = jax.nn.sigmoid(logits)
    gate_values = (
        (signal / jnp.sum(signal, axis=1, keepdims=True)).astype(jnp.bfloat16).astype(jnp.float32)
    )
    spread_sum = jnp.zeros((token_count, slot_count), jnp.float32)
    mixing_sum = jnp.zeros((token_count, slot_count), jnp.float32)
    for choice_index in range(TOPK):
        hit = slot_ids[None, :] == targets[:, choice_index : choice_index + 1]
        spread_sum = spread_sum + hit.astype(jnp.float32)
        mixing_sum = mixing_sum + jnp.where(
            hit, gate_values[:, choice_index : choice_index + 1], 0.0
        )
    spread = spread_sum.astype(jnp.bfloat16)
    mixing = mixing_sum.astype(jnp.bfloat16)
    outgoing = jnp.einsum(
        "ts,tw->sw", spread, token_rows, preferred_element_type=jnp.float32
    ).astype(jnp.bfloat16)
    outgoing = outgoing.reshape(columns, local_experts, capacity, feature_share)
    arrived = lax.all_to_all(outgoing, "expert", split_axis=0, concat_axis=0, tiled=True)
    arrived_wide = arrived.astype(jnp.float32)
    start_up = jnp.zeros((columns, local_experts, capacity, hidden_share), jnp.float32)
    squares = lax.psum(jnp.sum(jnp.square(arrived_wide), axis=3), "dp")
    gain_part = lax.dynamic_slice_in_dim(norm_gain, feature_index * feature_share, feature_share, 0)
    scaled = (arrived_wide * gain_part).astype(jnp.bfloat16)
    running = start_up
    piece = lax.all_gather(scaled, "dp", axis=3, tiled=True)
    start = jnp.int32(0)
    for block_number in range(piece.shape[3] // feature_share):
        first = block_number * feature_share
        running = running + block_product(
            piece[:, :, :, first : first + feature_share], w_up, start + first
        )
    inverse = 1.0 / jnp.sqrt(squares / D + NORM_EPSILON)
    projected = running * inverse[..., None]
    hidden = jnp.square(jnp.maximum(projected, 0.0)).astype(jnp.bfloat16)
    grad_term = attention_grad(
        queries[0], keys[0], values[0], out_grad[0], w_query, w_key, w_value, w_out, feature_index
    )
    grad_here = lax.psum_scatter(
        grad_term.astype(jnp.bfloat16), "dp", scatter_dimension=1, tiled=True
    )
    expert_out = jnp.einsum(
        "sjch,jhd->sjcd",
        lax.all_gather(hidden, "dp", axis=3, tiled=True),
        w_down,
        preferred_element_type=jnp.float32,
    )
    expert_rows = expert_out.astype(jnp.bfloat16)
    returned = lax.all_to_all(expert_rows, "expert", split_axis=0, concat_axis=0, tiled=True)
    moe_out = jnp.dot(
        mixing, returned.reshape(slot_count, feature_share), preferred_element_type=jnp.float32
    ).astype(jnp.bfloat16)
    moe_next, grad_prev = partner((moe_out, grad_here), "segment", 0)
    return (moe_next[None], grad_prev[None])


def solution(mesh):
    return jax.shard_map(
        on_device,
        mesh=mesh,
        in_specs=(
            P("segment", "expert", "dp"),
            P(),
            P("segment", "expert", None),
            P("segment", "expert", None),
            P("expert", None, "dp"),
            P("expert", None, "dp"),
            P("segment", "expert", "dp"),
            P("segment", "expert", None),
            P("segment", "expert", None),
            P("segment", "expert", None),
            P(None, "dp"),
            P(),
            P(),
            P("dp", None),
        ),
        out_specs=(P("segment", "expert", "dp"), P("segment", "expert", "dp")),
        check_vma=False,
    )
```

profile of v0, /device:TPU:0, one launch (start us, length us, event | category | flops | bytes accessed | tf_op | source)
XLA Modules:
  0.0 497.4 jit_solution(2547123518346177844)
XLA Ops:
  7.2 0.0 copy-start
  7.2 0.9 copy.82
  8.1 0.1 eq.120
  8.2 0.1 eq.116
  8.4 1.7 reduce-window.6
  10.1 0.3 slice_reduce_fusion.6
  10.4 0.1 fusion.79
  10.5 0.1 reshape.63
  10.6 0.3 slice_reduce_fusion.5
  10.9 0.0 copy-start.9
  10.9 0.0 copy-start.11
  11.0 0.0 copy-start.13
  11.0 0.5 copy-done.7
  11.4 0.0 copy-done.11
  11.5 0.0 copy-done.13
  11.5 3.5 convolution_convert_fusion
  15.0 21.9 %reshape.76 = bf16[8,2,54,1344]{2,1,0,3:T(2,128)(2,1)} reshape(bf16[864,1344]{0,1:T(8,128)(2,1)} %convolution_convert_fusion) | data formatting | bytes 4644864 | tf_op jit(solution)/shard_map/reshape | solution.py:143
  36.8 15.1 %copy.87 = bf16[8,2,54,1344]{3,1,2,0:T(2,128)(2,1)} copy(bf16[8,2,54,1344]{2,1,0,3:T(2,128)(2,1)} %reshape.76) | data formatting | bytes 4644864 | tf_op jit(solution)/shard_map/reshape | solution.py:143
  52.0 7.4 %all-to-all-start = ((bf16[8,2,54,1344]{3,1,2,0:T(2,128)(2,1)}), bf16[8,2,54,1344]{3,1,2,0:T(2,128)(2,1)}, u32[]{:S(2)}, u32[]{:S(2)}) async-start(bf16[8,2,54,1344]{3,1,2,0:T(2,128)(2,1)} %copy.87), calls=%async_computation | async-start | bytes 4866048 | tf_op jit(solution)/shard_map/all_to_all | solution.py:144
  59.4 0.0 all-gather.3.cloned.1.call-start
  59.5 0.1 dynamic_slice.25
  59.5 55.4 %all-to-all-done = bf16[8,2,54,1344]{3,1,2,0:T(2,128)(2,1)} async-done(((bf16[8,2,54,1344]{3,1,2,0:T(2,128)(2,1)}), bf16[8,2,54,1344]{3,1,2,0:T(2,128)(2,1)}, u32[]{:S(2)}, u32[]{:S(2)}) %all-to-all-start) | async-done | bytes 2322464 | tf_op jit(solution)/shard_map/all_to_all | solution.py:144
  114.9 3.9 fusion.13
  118.8 8.9 %copy.89 = bf16[8,2,54,1344]{2,0,1,3:T(8,128)(2,1)} copy(bf16[8,2,54,1344]{3,0,2,1:T(8,128)(2,1)} %get-tuple-element.11) | data formatting | bytes 4644864 | tf_op jit(solution)/shard_map/convert_element_type | solution.py:149
  127.7 0.0 all-gather.3.cloned.1.call-update
  127.8 0.0 all-gather.5.cloned.1.call-start
  127.8 0.1 copy.93
  127.9 5.0 psum.7
  132.9 129.3 %all-gather.3.cloned.1.call-done = bf16[8,2,54,2688]{2,0,1,3:T(8,128)(2,1)} async-done(((bf16[8,2,54,1344]{2,0,1,3:T(8,128)(2,1)}), bf16[8,2,54,2688]{2,0,1,3:T(8,128)(2,1)}) %all-gather.3.cloned.1.call-update) | async-done | bytes 4644880 | tf_op jit(solution)/shard_map/all_gather | solution.py:151
  262.2 5.5 %fusion.112 = (bf16[8,2,54,1344]{2,0,1,3:T(8,128)(2,1)S(1)}, bf16[8,2,54,1344]{2,0,1,3:T(8,128)(2,1)S(1)}) fusion(bf16[8,2,54,2688]{2,0,1,3:T(8,128)(2,1)} %all-gather.3.cloned.1.call-done), kind=kLoop, calls=%fused_computation.132 | loop fusion | bytes 9289728 | tf_op jit(solution)/shard_map/slice | solution.py:156
  267.7 11.1 %convert_bitcast_fusion.1 = bf16[8,2,54,928]{3,2,0,1:T(8,128)(2,1)} fusion(bf16[2,2688,928]{1,2,0:T(8,128)(2,1)} %param.18, bf16[8,2,54,1344]{2,0,1,3:T(8,128)(2,1)S(1)} %get-tuple-element.8), kind=kOutput, calls=%fused_computation.25 | convolution fusion | flops 2156018688 | bytes 9152512 | tf_op jit(solution)/shard_map/sjcw,jwh->sjch/dot_general | solution.py:84
  278.9 10.0 %convert_bitcast_fusion = bf16[8,2,54,928]{3,2,0,1:T(8,128)(2,1)S(1)} fusion(bf16[2,2688,928]{1,2,0:T(8,128)(2,1)} %param.18, bf16[8,2,54,1344]{2,0,1,3:T(8,128)(2,1)S(1)} %get-tuple-element.9), kind=kOutput, calls=%fused_computation.24 | convolution fusion | flops 2156018688 | bytes 9152512 | tf_op jit(solution)/shard_map/sjcw,jwh->sjch/dot_general | solution.py:84
  288.9 0.8 multiply_convert_fusion
  289.7 4.9 copy.94
  294.6 0.0 all-gather.5.cloned.1.call-update
  294.7 95.3 %all-gather.5.cloned.1.call-done = bf16[8,2,54,1856]{2,0,1,3:T(8,128)(2,1)} async-done(((bf16[8,2,54,928]{2,0,1,3:T(8,128)(2,1)}), bf16[8,2,54,1856]{2,0,1,3:T(8,128)(2,1)}) %all-gather.5.cloned.1.call-update) | async-done | bytes 3207184 | tf_op jit(solution)/shard_map/all_gather | solution.py:169
  389.9 20.2 %fusion.20 = bf16[8,2,54,1344]{3,2,0,1:T(8,128)(2,1)} fusion(bf16[2,1856,1344]{1,2,0:T(8,128)(2,1)} %param.19, bf16[8,2,54,1856]{2,0,1,3:T(8,128)(2,1)} %all-gather.5.cloned.1.call-done), kind=kOutput, calls=%fused_computation.22 | convolution fusion | flops 4311595008 | bytes 15507456 | tf_op jit(solution)/shard_map/sjch,jhd->sjcd/dot_general | solution.py:167
  410.1 5.7 %copy.96 = bf16[8,2,54,1344]{3,1,2,0:T(2,128)(2,1)} copy(bf16[8,2,54,1344]{3,2,0,1:T(8,128)(2,1)} %fusion.20) | data formatting | bytes 4644864 | tf_op jit(solution)/shard_map/convert_element_type | solution.py:173
  415.8 5.6 %all-to-all-start.1 = ((bf16[8,2,54,1344]{3,1,2,0:T(2,128)(2,1)}), bf16[8,2,54,1344]{3,1,2,0:T(2,128)(2,1)}, u32[]{:S(2)}, u32[]{:S(2)}) async-start(bf16[8,2,54,1344]{3,1,2,0:T(2,128)(2,1)} %copy.96), calls=%async_computation.1 | async-start | bytes 4866048 | tf_op jit(solution)/shard_map/all_to_all | solution.py:174
  421.4 0.3 reduce-scatter.2.cloned.1.call-start
  421.8 0.0 copy-done.4
  421.8 0.0 copy-start.15
  421.9 0.3 fusion.113
  422.2 4.4 fusion.38
  426.6 0.0 copy-done.15
  426.6 0.2 multiply_reduce_fusion
  426.9 0.1 multiply_convert_fusion.1
  427.0 1.0 fusion.37
  427.9 1.6 fusion.42
  429.6 4.6 convolution_add_fusion
  434.2 0.0 copy-start.6
  434.2 2.5 fusion.14
  436.8 0.0 reduce-scatter.2.cloned.1.call-update
  436.9 16.7 %reduce-scatter.2.cloned.1.call-done = bf16[128,1344]{0,1:T(8,128)(2,1)} async-done(((bf16[128,2688]{0,1:T(8,128)(2,1)}), bf16[128,1344]{0,1:T(8,128)(2,1)}) %reduce-scatter.2.cloned.1.call-update) | async-done | bytes 344080 | tf_op jit(solution)/shard_map/reduce_scatter | solution.py:164
  453.5 0.0 collective-permute-start.1
  453.5 23.2 %all-to-all-done.1 = bf16[8,2,54,1344]{3,1,2,0:T(2,128)(2,1)} async-done(((bf16[8,2,54,1344]{3,1,2,0:T(2,128)(2,1)}), bf16[8,2,54,1344]{3,1,2,0:T(2,128)(2,1)}, u32[]{:S(2)}, u32[]{:S(2)}) %all-to-all-start.1) | async-done | bytes 2322464 | tf_op jit(solution)/shard_map/all_to_all | solution.py:174
  476.8 3.5 copy.97
  480.3 4.4 reshape.65
  484.7 3.0 convolution_convert_fusion.1
  487.7 0.1 collective-permute-start
  487.8 0.0 collective-permute-done.1
  487.8 1.6 collective-permute-done
  489.4 0.7 copy.171
  490.2 0.7 copy.172
  (31 shorter events, 0.2 us)
Async XLA Ops:
  7.2 420.8 %copy-start = (bf16[2688,256]{1,0:T(8,128)(2,1)S(1)}, bf16[2688,256]{1,0:T(8,128)(2,1)}, u32[]{:S(2)}) copy-start(bf16[2688,256]{1,0:T(8,128)(2,1)} %param.25) | copy-start | bytes 4128772
  10.9 0.5 copy-start.7
  10.9 0.5 copy-start.9
  10.9 0.5 copy-start.11
  11.0 0.6 copy-start.13
  51.9 7.5 %copy-start.5 = (f32[2688]{0:T(1024)S(1)}, f32[2688]{0:T(1024)}, u32[]{:S(2)}) copy-start(f32[2688]{0:T(1024)} %param.15) | copy-start | bytes 32260
  52.0 63.0 %all-to-all-start = ((bf16[8,2,54,1344]{3,1,2,0:T(2,128)(2,1)}), bf16[8,2,54,1344]{3,1,2,0:T(2,128)(2,1)}, u32[]{:S(2)}, u32[]{:S(2)}) async-start(bf16[8,2,54,1344]{3,1,2,0:T(2,128)(2,1)} %copy.87), calls=%async_computation | async-start | bytes 4866048 | tf_op jit(solution)/shard_map/all_to_all | solution.py:144
  59.4 202.8 %all-gather.3.cloned.1.call-start = ((), (), s32[]{:S(2)}) async-start(), calls=%async_computation.3 | async-start | bytes 16515072 | tf_op jit(solution)/shard_map/all_gather | solution.py:151
  127.8 262.2 %all-gather.5.cloned.1.call-start = ((), (), s32[]{:S(2)}) async-start(), calls=%async_computation.4 | async-start | bytes 11403264 | tf_op jit(solution)/shard_map/all_gather | solution.py:169
  278.9 10.1 %copy-start.1 = (bf16[8,2,54,928]{3,2,0,1:T(8,128)(2,1)S(1)}, bf16[8,2,54,928]{3,2,0,1:T(8,128)(2,1)}, u32[]{:S(2)}) copy-start(bf16[8,2,54,928]{3,2,0,1:T(8,128)(2,1)} %convert_bitcast_fusion.1) | copy-start | bytes 4810756
  415.8 6.0 %copy-start.3 = (bf16[1,128,1024]{2,1,0:T(8,128)(2,1)S(1)}, bf16[1,128,1024]{2,1,0:T(8,128)(2,1)}, u32[]{:S(2)}) copy-start(bf16[1,128,1024]{2,1,0:T(8,128)(2,1)} %param.20) | copy-start | bytes 786436
  415.8 6.1 %copy-start.4 = (bf16[1,128,256]{2,1,0:T(8,128)(2,1)S(1)}, bf16[1,128,256]{2,1,0:T(8,128)(2,1)}, u32[]{:S(2)}) copy-start(bf16[1,128,256]{2,1,0:T(8,128)(2,1)} %param.21) | copy-start | bytes 196612
  415.8 6.4 %copy-start.2 = (bf16[1,128,2688]{2,1,0:T(8,128)(2,1)S(1)}, bf16[1,128,2688]{2,1,0:T(8,128)(2,1)}, u32[]{:S(2)}) copy-start(bf16[1,128,2688]{2,1,0:T(8,128)(2,1)} %param.23) | copy-start | bytes 2064388
  415.8 61.0 %all-to-all-start.1 = ((bf16[8,2,54,1344]{3,1,2,0:T(2,128)(2,1)}), bf16[8,2,54,1344]{3,1,2,0:T(2,128)(2,1)}, u32[]{:S(2)}, u32[]{:S(2)}) async-start(bf16[8,2,54,1344]{3,1,2,0:T(2,128)(2,1)} %copy.96), calls=%async_computation.1 | async-start | bytes 4866048 | tf_op jit(solution)/shard_map/all_to_all | solution.py:174
  421.4 32.1 %reduce-scatter.2.cloned.1.call-start = ((), (), s32[]{:S(2)}) async-start(), calls=%async_computation.5 | async-start | bytes 1032192 | tf_op jit(solution)/shard_map/reduce_scatter | solution.py:164
  421.8 4.8 copy-start.15
  434.2 2.6 copy-start.6
  453.5 34.3 %collective-permute-start.1 = (bf16[128,1344]{0,1:T(8,128)(2,1)}, bf16[128,1344]{0,1:T(8,128)(2,1)S(1)}, u32[]{:S(2)}, u32[]{:S(2)}) collective-permute-start(bf16[128,1344]{0,1:T(8,128)(2,1)} %reduce-scatter.2.cloned.1.call-done), channel_id=1, source_target_pairs={{0,16},{16,0},{1,17},{17,1},{2,18},{18,2},{3,19},{19,3},{4,20},{20... | collective-permute-start | bytes 1032200 | tf_op jit(solution)/shard_map/ppermute | solution.py:21
  480.3 4.4 copy-start.8
  480.3 4.4 copy-start.10
  480.3 4.4 copy-start.12
  480.3 4.4 copy-start.14
  487.7 1.7 collective-permute-start
Sparse Core Ops, SparseCore 0:
  127.9 134.2 all-gather.2
  294.8 95.1 all-gather.4
  436.9 16.5 reduce-scatter.1
where the time goes:
time: 499 us; the launch traced here: 497 us
  waiting for transfers between devices  322 us (65%)
  local copies, waits for them, and re-layouts  74 us (15%)
  matrix products  62.6 us (13%)
  between operations  14.1 us (3%)
  starting transfers between devices  13.5 us (3%)
  other arithmetic  6.66 us (1%)
    all_gather x1, waiting for transfers between devices, on_device(): piece = lax.all_gather(scaled, 'dp', axis=3, tiled=True)  129 us
    all_gather x1, waiting for transfers between devices, on_device(): lax.all_gather(hidden, 'dp', axis=3, tiled=True)  95.3 us
    all_to_all x1, waiting for transfers between devices, on_device(): lax.all_to_all(outgoing, 'expert', split_axis=0, concat_axis=0, tiled=True)  55.4 us
    reshape x2, local copies, waits for them, and re-layouts, on_device(): outgoing = outgoing.reshape(columns, local_experts, capacity, feature_share)  37 us
    all_to_all x1, waiting for transfers between devices, on_device(): lax.all_to_all(expert_rows, 'expert', split_axis=0, concat_axis=0, tiled=...  23.2 us
    dot_general x2, matrix products, block_product(): jnp.einsum('sjcw,jwh->sjch', block_rows, weight_rows, preferred_element_t...  21.2 us
    dot_general x1, matrix products, on_device(): jnp.einsum('sjch,jhd->sjcd', lax.all_gather(hidden, 'dp', axis=3, tiled=T...  20.2 us
    reduce_scatter x1, waiting for transfers between devices, on_device(): lax.psum_scatter(grad_term.astype(jnp.bfloat16), 'dp', scatter_dimension=...  16.7 us
  transfers between devices with their start and end apart: 7, of which 6 were waited for; matrix products, arithmetic and copies ran while one was open for 5% of the time, Pallas kernels for 0%

commit v1 on v0

--- a/solution.py
+++ b/solution.py
@@ -9,6 +9,30 @@
 HEAD_DIM = 128
 TOPK = 6
 NORM_EPSILON = 1e-05
+
+
+def split_up(x, dim, size):
+    shape = x.shape
+    parts = x.reshape(*shape[:dim], size, shape[dim] // size, *shape[dim + 1 :])
+    return jnp.moveaxis(parts, dim, 0)
+
+
+def in_order(tiles, dim):
+    dims = list(tiles.shape[1:])
+    dims[dim] *= tiles.shape[0]
+    return jnp.moveaxis(tiles, 0, dim).reshape(dims)
+
+
+def rotated_exchange(shard, axis, split_dim, concat_dim):
+    length, mine = (lax.axis_size(axis), lax.axis_index(axis))
+    tiles = split_up(shard, split_dim, length)
+    out = tiles
+    for step in range(1, length):
+        target, source = ((mine + step) % length, (mine - step) % length)
+        sent = lax.dynamic_index_in_dim(tiles, target, 0)
+        theirs = lax.ppermute(sent, axis, [(i, (i + step) % length) for i in range(length)])
+        out = lax.dynamic_update_slice_in_dim(out, theirs, source, axis=0)
+    return in_order(out, concat_dim)
 
 
 def partner(block, axis, distance):
@@ -141,7 +165,7 @@
         "ts,tw->sw", spread, token_rows, preferred_element_type=jnp.float32
     ).astype(jnp.bfloat16)
     outgoing = outgoing.reshape(columns, local_experts, capacity, feature_share)
-    arrived = lax.all_to_all(outgoing, "expert", split_axis=0, concat_axis=0, tiled=True)
+    arrived = rotated_exchange(outgoing, "expert", 0, 0)
     arrived_wide = arrived.astype(jnp.float32)
     start_up = jnp.zeros((columns, local_experts, capacity, hidden_share), jnp.float32)
     squares = lax.psum(jnp.sum(jnp.square(arrived_wide), axis=3), "dp")

time: 499 us -> 474 us (0.950)
  waiting for transfers between devices: 322 us -> 300 us
  local copies, waits for them, and re-layouts: 74 us -> 61.5 us
  starting transfers between devices: 13.5 us -> 22.7 us
    all_to_all x1 -> x0, waiting for transfers between devices: 55.4 us -> none  [on_device(): lax.all_to_all(outgoing, 'expert', split_axis=0, concat_axis=0, tiled=True)]
    reshape x2 -> x1, local copies, waits for them, and re-layouts: 37 us -> 4.2 us  [in_order(): return jnp.moveaxis(tiles, 0, dim).reshape(dims)]
    all_gather x1, waiting for transfers between devices: 129 us -> 147 us  [on_device(): piece = lax.all_gather(scaled, 'dp', axis=3, tiled=True)]
    ppermute x0 -> x7, waiting for transfers between devices: none -> 16.6 us  [rotated_exchange(): lax.ppermute(sent, axis, [(i, (i + step) % length) for i in range(length)])]
    ppermute x0 -> x7, starting transfers between devices: none -> 16.6 us  [rotated_exchange(): lax.ppermute(sent, axis, [(i, (i + step) % length) for i in range(length)])]
    dynamic_update_slice x0 -> x7, local copies, waits for them, and re-layouts: none -> 10.1 us  [rotated_exchange(): out = lax.dynamic_update_slice_in_dim(out, theirs, source, axis=0)]
    all_to_all x1 -> x0, starting transfers between devices: 7.44 us -> none  [on_device(): lax.all_to_all(outgoing, 'expert', split_axis=0, concat_axis=0, tiled=True)]
  transfers between devices with their start and end apart: 7 -> 13, of which waited for: 6 -> 6; matrix products, arithmetic and copies ran while one was open for 5% -> 8% of each run, Pallas kernels for 0% -> 0%
where the time goes in v1:
time: 474 us; the launch traced here: 473 us
  waiting for transfers between devices  300 us (63%)
  matrix products  62.7 us (13%)
  local copies, waits for them, and re-layouts  61.5 us (13%)
  starting transfers between devices  22.7 us (5%)
  between operations  14.2 us (3%)
  other arithmetic  6.74 us (1%)
  blocking collectives  5 us (1%)
    all_gather x1, waiting for transfers between devices, on_device(): piece = lax.all_gather(scaled, 'dp', axis=3, tiled=True)  147 us
    all_gather x1, waiting for transfers between devices, on_device(): lax.all_gather(hidden, 'dp', axis=3, tiled=True)  95.3 us
    all_to_all x1, waiting for transfers between devices, on_device(): lax.all_to_all(expert_rows, 'expert', split_axis=0, concat_axis=0, tiled=...  23.2 us
    dot_general x2, matrix products, block_product(): jnp.einsum('sjcw,jwh->sjch', block_rows, weight_rows, preferred_element_t...  21.2 us
    dot_general x1, matrix products, on_device(): jnp.einsum('sjch,jhd->sjcd', lax.all_gather(hidden, 'dp', axis=3, tiled=T...  20.2 us
    reduce_scatter x1, waiting for transfers between devices, on_device(): lax.psum_scatter(grad_term.astype(jnp.bfloat16), 'dp', scatter_dimension=...  16.7 us
    ppermute x7, waiting for transfers between devices, rotated_exchange(): lax.ppermute(sent, axis, [(i, (i + step) % length) for i in range(length)])  16.6 us
    ppermute x7, starting transfers between devices, rotated_exchange(): lax.ppermute(sent, axis, [(i, (i + step) % length) for i in range(length)])  16.6 us
  transfers between devices with their start and end apart: 13, of which 6 were waited for; matrix products, arithmetic and copies ran while one was open for 8% of the time, Pallas kernels for 0%

profile of v1, /device:TPU:0, one launch (start us, length us, event | category | flops | bytes accessed | tf_op | source)
XLA Modules:
  0.0 473.2 jit_solution(16640605087813781126)
XLA Ops:
  7.2 0.0 all-gather.3.cloned.1.call-start
  7.3 0.9 copy.119
  8.2 0.1 eq.135
  8.3 0.1 eq.131
  8.5 1.7 reduce-window.6
  10.2 0.3 slice_reduce_fusion.6
  10.5 0.1 fusion.79
  10.6 0.1 reshape.92
  10.7 0.3 slice_reduce_fusion.5
  11.1 0.5 copy-done.7
  11.6 0.0 copy-done.13
  11.6 3.5 convolution_convert_fusion
  15.1 4.4 copy.123
  19.5 4.2 reshape_reshape.3
  23.7 2.4 constant_dynamic-slice_fusion
  26.1 3.0 collective-permute-start
  29.1 1.6 collective-permute-start.1
  30.7 2.5 collective-permute-start.2
  33.2 1.2 collective-permute-start.3
  34.4 2.6 collective-permute-start.4
  37.1 4.2 reshape.93
  41.3 0.1 dynamic_slice.54
  41.4 1.3 collective-permute-start.5
  42.7 1.7 bitcast_dynamic-update-slice_fusion.6
  44.4 4.3 collective-permute-start.6
  48.7 1.7 bitcast_dynamic-update-slice_fusion.5
  50.4 16.6 %collective-permute-done.2 = bf16[1,1,2,54,1344]{4,3,2,1,0:T(8,128)(2,1)} collective-permute-done((bf16[1,1,2,54,1344]{4,3,2,1,0:T(8,128)(2,1)S(1)}, bf16[1,1,2,54,1344]{4,3,2,1,0:T(8,128)(2,1)}, u32[]{:S(2)}, u32[]{:S(2)}) %collective-permute-start.2) | collective-permute-done | bytes 290336 | tf_op jit(solution)/shard_map/ppermute | solution.py:33
  67.1 1.7 bitcast_dynamic-update-slice_fusion.4
  68.8 1.7 bitcast_dynamic-update-slice_fusion.3
  70.5 1.7 bitcast_dynamic-update-slice_fusion.2
  72.2 0.7 bitcast_dynamic-update-slice_fusion.1
  73.0 0.7 bitcast_dynamic-update-slice_fusion
  73.7 4.0 fusion.13
  77.7 8.3 %copy.132 = bf16[8,2,54,1344]{2,0,1,3:T(8,128)(2,1)} copy(bf16[8,2,54,1344]{3,2,1,0:T(8,128)(2,1)} %get-tuple-element.11) | data formatting | bytes 4644864 | tf_op jit(solution)/shard_map/convert_element_type | solution.py:173
  86.0 0.0 all-gather.5.cloned.1.call-start
  86.0 5.0 %psum.7 = f32[8,2,54]{2,0,1:T(8,128)S(1)} all-reduce(f32[8,2,54]{2,0,1:T(8,128)S(1)} %copy.135), channel_id=1, replica_groups=mesh['segment'=2,'expert'=8,'dp'=2] {'dp'}, use_global_device_ids=true, to_apply=%region_5.6 | all-reduce | flops 864 | bytes 6912 | tf_op jit(solution)/shard_map/psum | solution.py:171
  91.0 147.0 %all-gather.3.cloned.1.call-done = bf16[8,2,54,2688]{2,0,1,3:T(8,128)(2,1)} async-done(((bf16[8,2,54,1344]{2,0,1,3:T(8,128)(2,1)}), bf16[8,2,54,2688]{2,0,1,3:T(8,128)(2,1)}) %all-gather.3.cloned.1.call-update) | async-done | bytes 4644880 | tf_op jit(solution)/shard_map/all_gather | solution.py:175
  238.0 5.5 %fusion.112 = (bf16[8,2,54,1344]{2,0,1,3:T(8,128)(2,1)S(1)}, bf16[8,2,54,1344]{2,0,1,3:T(8,128)(2,1)S(1)}) fusion(bf16[8,2,54,2688]{2,0,1,3:T(8,128)(2,1)} %all-gather.3.cloned.1.call-done), kind=kLoop, calls=%fused_computation.146 | loop fusion | bytes 9289728 | tf_op jit(solution)/shard_map/slice | solution.py:180
  243.5 11.1 %convert_bitcast_fusion.1 = bf16[8,2,54,928]{3,2,0,1:T(8,128)(2,1)} fusion(bf16[2,2688,928]{1,2,0:T(8,128)(2,1)} %param.18, bf16[8,2,54,1344]{2,0,1,3:T(8,128)(2,1)S(1)} %get-tuple-element.8), kind=kOutput, calls=%fused_computation.25 | convolution fusion | flops 2156018688 | bytes 9152512 | tf_op jit(solution)/shard_map/sjcw,jwh->sjch/dot_general | solution.py:108
  254.7 10.0 %convert_bitcast_fusion = bf16[8,2,54,928]{3,2,0,1:T(8,128)(2,1)S(1)} fusion(bf16[2,2688,928]{1,2,0:T(8,128)(2,1)} %param.18, bf16[8,2,54,1344]{2,0,1,3:T(8,128)(2,1)S(1)} %get-tuple-element.9), kind=kOutput, calls=%fused_computation.24 | convolution fusion | flops 2156018688 | bytes 9152512 | tf_op jit(solution)/shard_map/sjcw,jwh->sjch/dot_general | solution.py:108
  264.7 0.8 multiply_convert_fusion
  265.5 4.9 %copy.136 = bf16[8,2,54,928]{2,0,1,3:T(8,128)(2,1)} copy(bf16[8,2,54,928]{3,2,0,1:T(8,128)(2,1)S(1)} %multiply_convert_fusion) | data formatting | bytes 3207168 | tf_op jit(solution)/shard_map/convert_element_type | solution.py:184
  270.5 95.3 %all-gather.5.cloned.1.call-done = bf16[8,2,54,1856]{2,0,1,3:T(8,128)(2,1)} async-done(((bf16[8,2,54,928]{2,0,1,3:T(8,128)(2,1)}), bf16[8,2,54,1856]{2,0,1,3:T(8,128)(2,1)}) %all-gather.5.cloned.1.call-update) | async-done | bytes 3207184 | tf_op jit(solution)/shard_map/all_gather | solution.py:193
  365.7 20.2 %fusion.20 = bf16[8,2,54,1344]{3,2,0,1:T(8,128)(2,1)} fusion(bf16[2,1856,1344]{1,2,0:T(8,128)(2,1)} %param.19, bf16[8,2,54,1856]{2,0,1,3:T(8,128)(2,1)} %all-gather.5.cloned.1.call-done), kind=kOutput, calls=%fused_computation.22 | convolution fusion | flops 4311595008 | bytes 15507456 | tf_op jit(solution)/shard_map/sjch,jhd->sjcd/dot_general | solution.py:191
  385.9 5.7 %copy.138 = bf16[8,2,54,1344]{3,1,2,0:T(2,128)(2,1)} copy(bf16[8,2,54,1344]{3,2,0,1:T(8,128)(2,1)} %fusion.20) | data formatting | bytes 4644864 | tf_op jit(solution)/shard_map/convert_element_type | solution.py:197
  391.6 5.6 %all-to-all-start = ((bf16[8,2,54,1344]{3,1,2,0:T(2,128)(2,1)}), bf16[8,2,54,1344]{3,1,2,0:T(2,128)(2,1)}, u32[]{:S(2)}, u32[]{:S(2)}) async-start(bf16[8,2,54,1344]{3,1,2,0:T(2,128)(2,1)} %copy.138), calls=%async_computation | async-start | bytes 4866048 | tf_op jit(solution)/shard_map/all_to_all | solution.py:198
  397.2 0.3 reduce-scatter.2.cloned.1.call-start
  397.7 0.3 fusion.113
  398.0 4.5 fusion.38
  402.5 0.2 multiply_reduce_fusion
  402.8 0.1 multiply_convert_fusion.1
  402.8 1.0 fusion.37
  403.8 1.6 fusion.42
  405.4 4.6 convolution_add_fusion
  410.1 2.5 fusion.14
  412.7 16.7 %reduce-scatter.2.cloned.1.call-done = bf16[128,1344]{0,1:T(8,128)(2,1)} async-done(((bf16[128,2688]{0,1:T(8,128)(2,1)}), bf16[128,1344]{0,1:T(8,128)(2,1)}) %reduce-scatter.2.cloned.1.call-update) | async-done | bytes 344080 | tf_op jit(solution)/shard_map/reduce_scatter | solution.py:188
  429.4 23.2 %all-to-all-done = bf16[8,2,54,1344]{3,1,2,0:T(2,128)(2,1)} async-done(((bf16[8,2,54,1344]{3,1,2,0:T(2,128)(2,1)}), bf16[8,2,54,1344]{3,1,2,0:T(2,128)(2,1)}, u32[]{:S(2)}, u32[]{:S(2)}) %all-to-all-start) | async-done | bytes 2322464 | tf_op jit(solution)/shard_map/all_to_all | solution.py:198
  452.6 3.5 copy.139
  456.1 4.4 reshape.101
  460.5 3.0 convolution_convert_fusion.1
  463.5 0.1 collective-permute-start.7
  463.6 1.6 collective-permute-done.7
  465.2 0.7 copy.214
  466.0 0.7 copy.215
  (52 shorter events, 0.3 us)
Async XLA Ops:
  7.2 396.6 %copy-start = (bf16[2688,256]{1,0:T(8,128)(2,1)S(1)}, bf16[2688,256]{1,0:T(8,128)(2,1)}, u32[]{:S(2)}) copy-start(bf16[2688,256]{1,0:T(8,128)(2,1)} %param.25) | copy-start | bytes 4128772
  7.2 230.8 %all-gather.3.cloned.1.call-start = ((), (), s32[]{:S(2)}) async-start(), calls=%async_computation.2 | async-start | bytes 16515072 | tf_op jit(solution)/shard_map/all_gather | solution.py:175
  11.0 0.5 copy-start.7
  11.0 0.5 copy-start.9
  11.1 0.5 copy-start.11
  11.1 0.6 copy-start.13
  26.1 15.3 %collective-permute-start = (bf16[1,1,2,54,1344]{4,3,2,1,0:T(8,128)(2,1)}, bf16[1,1,2,54,1344]{4,3,2,1,0:T(8,128)(2,1)}, u32[]{:S(2)}, u32[]{:S(2)}) collective-permute-start(bf16[1,1,2,54,1344]{4,3,2,1,0:T(8,128)(2,1)} %get-tuple-element.18), channel_id=1, source_target_pairs={{0,2},{2,4},{4,6},{6,8},{8,10},{10,12},{12,14},{14,0},{1,3},{3,5},... | collective-permute-start | bytes 870920 | tf_op jit(solution)/shard_map/ppermute | solution.py:33
  29.1 15.3 %collective-permute-start.1 = (bf16[1,1,2,54,1344]{4,3,2,1,0:T(8,128)(2,1)S(1)}, bf16[1,1,2,54,1344]{4,3,2,1,0:T(8,128)(2,1)}, u32[]{:S(2)}, u32[]{:S(2)}) collective-permute-start(bf16[1,1,2,54,1344]{4,3,2,1,0:T(8,128)(2,1)S(1)} %get-tuple-element.17), channel_id=1, source_target_pairs={{0,4},{2,6},{4,8},{6,10},{8,12},{10,14},{12,0},{14,2},{1,5},{3,7},... | collective-permute-start | bytes 870920 | tf_op jit(solution)/shard_map/ppermute | solution.py:33
  30.7 36.4 %collective-permute-start.2 = (bf16[1,1,2,54,1344]{4,3,2,1,0:T(8,128)(2,1)S(1)}, bf16[1,1,2,54,1344]{4,3,2,1,0:T(8,128)(2,1)}, u32[]{:S(2)}, u32[]{:S(2)}) collective-permute-start(bf16[1,1,2,54,1344]{4,3,2,1,0:T(8,128)(2,1)S(1)} %get-tuple-element.16), channel_id=1, source_target_pairs={{0,6},{2,8},{4,10},{6,12},{8,14},{10,0},{12,2},{14,4},{1,7},{3,9},... | collective-permute-start | bytes 870920 | tf_op jit(solution)/shard_map/ppermute | solution.py:33
  33.2 35.6 %collective-permute-start.3 = (bf16[1,1,2,54,1344]{4,3,2,1,0:T(8,128)(2,1)S(1)}, bf16[1,1,2,54,1344]{4,3,2,1,0:T(8,128)(2,1)}, u32[]{:S(2)}, u32[]{:S(2)}) collective-permute-start(bf16[1,1,2,54,1344]{4,3,2,1,0:T(8,128)(2,1)S(1)} %get-tuple-element.15), channel_id=1, source_target_pairs={{0,8},{2,10},{4,12},{6,14},{8,0},{10,2},{12,4},{14,6},{1,9},{3,11}... | collective-permute-start | bytes 870920 | tf_op jit(solution)/shard_map/ppermute | solution.py:33
  34.4 36.1 %collective-permute-start.4 = (bf16[1,1,2,54,1344]{4,3,2,1,0:T(8,128)(2,1)S(1)}, bf16[1,1,2,54,1344]{4,3,2,1,0:T(8,128)(2,1)}, u32[]{:S(2)}, u32[]{:S(2)}) collective-permute-start(bf16[1,1,2,54,1344]{4,3,2,1,0:T(8,128)(2,1)S(1)} %get-tuple-element.14), channel_id=1, source_target_pairs={{0,10},{2,12},{4,14},{6,0},{8,2},{10,4},{12,6},{14,8},{1,11},{3,13... | collective-permute-start | bytes 870920 | tf_op jit(solution)/shard_map/ppermute | solution.py:33
  37.1 4.2 copy-start.5
  41.4 30.9 %collective-permute-start.5 = (bf16[1,1,2,54,1344]{4,3,2,1,0:T(8,128)(2,1)S(1)}, bf16[1,1,2,54,1344]{4,3,2,1,0:T(8,128)(2,1)S(1)}, u32[]{:S(2)}, u32[]{:S(2)}) collective-permute-start(bf16[1,1,2,54,1344]{4,3,2,1,0:T(8,128)(2,1)S(1)} %get-tuple-element.13), channel_id=1, source_target_pairs={{0,12},{2,14},{4,0},{6,2},{8,4},{10,6},{12,8},{14,10},{1,13},{3,15... | collective-permute-start | bytes 870920 | tf_op jit(solution)/shard_map/ppermute | solution.py:33
  44.4 28.6 %collective-permute-start.6 = (bf16[1,1,2,54,1344]{4,3,2,1,0:T(8,128)(2,1)S(1)}, bf16[1,1,2,54,1344]{4,3,2,1,0:T(8,128)(2,1)S(1)}, u32[]{:S(2)}, u32[]{:S(2)}) collective-permute-start(bf16[1,1,2,54,1344]{4,3,2,1,0:T(8,128)(2,1)S(1)} %get-tuple-element.12), channel_id=1, source_target_pairs={{0,14},{2,0},{4,2},{6,4},{8,6},{10,8},{12,10},{14,12},{1,15},{3,1}... | collective-permute-start | bytes 870920 | tf_op jit(solution)/shard_map/ppermute | solution.py:33
  86.0 279.8 %all-gather.5.cloned.1.call-start = ((), (), s32[]{:S(2)}) async-start(), calls=%async_computation.3 | async-start | bytes 11403264 | tf_op jit(solution)/shard_map/all_gather | solution.py:193
  254.7 10.1 %copy-start.1 = (bf16[8,2,54,928]{3,2,0,1:T(8,128)(2,1)S(1)}, bf16[8,2,54,928]{3,2,0,1:T(8,128)(2,1)}, u32[]{:S(2)}) copy-start(bf16[8,2,54,928]{3,2,0,1:T(8,128)(2,1)} %convert_bitcast_fusion.1) | copy-start | bytes 4810756
  391.6 6.0 %copy-start.3 = (bf16[1,128,1024]{2,1,0:T(8,128)(2,1)S(1)}, bf16[1,128,1024]{2,1,0:T(8,128)(2,1)}, u32[]{:S(2)}) copy-start(bf16[1,128,1024]{2,1,0:T(8,128)(2,1)} %param.20) | copy-start | bytes 786436
  391.6 6.1 %copy-start.4 = (bf16[1,128,256]{2,1,0:T(8,128)(2,1)S(1)}, bf16[1,128,256]{2,1,0:T(8,128)(2,1)}, u32[]{:S(2)}) copy-start(bf16[1,128,256]{2,1,0:T(8,128)(2,1)} %param.21) | copy-start | bytes 196612
  391.6 6.4 %copy-start.2 = (bf16[1,128,2688]{2,1,0:T(8,128)(2,1)S(1)}, bf16[1,128,2688]{2,1,0:T(8,128)(2,1)}, u32[]{:S(2)}) copy-start(bf16[1,128,2688]{2,1,0:T(8,128)(2,1)} %param.23) | copy-start | bytes 2064388
  391.6 61.0 %all-to-all-start = ((bf16[8,2,54,1344]{3,1,2,0:T(2,128)(2,1)}), bf16[8,2,54,1344]{3,1,2,0:T(2,128)(2,1)}, u32[]{:S(2)}, u32[]{:S(2)}) async-start(bf16[8,2,54,1344]{3,1,2,0:T(2,128)(2,1)} %copy.138), calls=%async_computation | async-start | bytes 4866048 | tf_op jit(solution)/shard_map/all_to_all | solution.py:198
  397.2 32.2 %reduce-scatter.2.cloned.1.call-start = ((), (), s32[]{:S(2)}) async-start(), calls=%async_computation.4 | async-start | bytes 1032192 | tf_op jit(solution)/shard_map/reduce_scatter | solution.py:188
  398.0 4.5 copy-start.15
  410.1 2.6 copy-start.6
  429.4 34.2 %collective-permute-start.8 = (bf16[128,1344]{0,1:T(8,128)(2,1)}, bf16[128,1344]{0,1:T(8,128)(2,1)S(1)}, u32[]{:S(2)}, u32[]{:S(2)}) collective-permute-start(bf16[128,1344]{0,1:T(8,128)(2,1)} %reduce-scatter.2.cloned.1.call-done), channel_id=1, source_target_pairs={{0,16},{16,0},{1,17},{17,1},{2,18},{18,2},{3,19},{19,3},{4,20},{20... | collective-permute-start | bytes 1032200 | tf_op jit(solution)/shard_map/ppermute | solution.py:45
  456.1 4.4 copy-start.8
  456.1 4.4 copy-start.10
  456.1 4.4 copy-start.12
  456.1 4.4 copy-start.14
  463.5 1.7 collective-permute-start.7
Sparse Core Ops, SparseCore 0:
  86.1 151.8 all-gather.2
  270.6 95.1 all-gather.4
  412.8 16.5 reduce-scatter.1
